TPU v7x, 32 devices: a whole 2x2x4 slice. The times are simulated.
32 devices in a mesh: grp: 2 (over y), blk: 8 (over z, x), seq: 1, ch: 2 (over core).
Axes of the slice: x: 2, y: 2, z: 4, core: 2. Of those that a mesh axis runs over, the one named last changes fastest.
Arguments:
- alignment_activity: bfloat16 [512, 128, 64], P(('grp', 'seq'), 'blk'), parts along dimension 0, may hold values from -40 to 40
- sequence_mask: int32 [512], P('grp'), parts along dimension 0, may hold values 0 or 1
- residue_mask: int32 [256], P('grp'), parts along dimension 0, may hold values 0 or 1
- lower_weights: bfloat16 [64, 32], replicated, may hold values from -0.75 to 0.75
- upper_weights: bfloat16 [64, 32], replicated, may hold values from -0.75 to 0.75
- output_projector: bfloat16 [1024, 128], replicated, may hold values from -0.1875 to 0.1875
Outputs:
- pair_update: bfloat16 [128, 256, 128], P('ch', ('grp', 'blk'), 'seq'), parts along dimension 1
There are 2 independent parts, one for each index of `grp`. A program takes and returns all parts, laid end to end along the dimension named above; an argument that names none is the same for every part. Nothing has to cross between parts.
All inputs are finite; a program needn't handle non-finite values.
Results may differ from a plain program's by a relative error of at most 0.012.
Values may be sent and summed in bfloat16 or wider, within the bound.
A program may use at most 64 MiB of HBM per device.

v0:
```python
import math
import jax
import jax.numpy as jnp
from jax import lax
from jax.sharding import PartitionSpec as P


def shards(
    alignment_activity, sequence_mask, residue_mask, lower_weights, upper_weights, output_projector
):
    local_rows, block_rows, channel_count = alignment_activity.shape
    proj_width = lower_weights.shape[1]
    pair_width = output_projector.shape[1]
    seq_count = lax.axis_size("seq")
    core_count = lax.axis_size("ch")
    seq_place = lax.axis_index("seq")
    blk_place = lax.axis_index("blk")
    core_place = lax.axis_index("ch")
    value_entries = alignment_activity.astype(jnp.float32)
    centred = value_entries - jnp.mean(value_entries, axis=-1, keepdims=True)
    variance = jnp.mean(centred * centred, axis=-1, keepdims=True)
    normed = (centred * lax.rsqrt(variance + 1e-05)).astype(jnp.bfloat16)
    rows_valid = lax.dynamic_slice_in_dim(sequence_mask, seq_place * local_rows, local_rows).astype(
        jnp.float32
    )
    res_valid = lax.dynamic_slice_in_dim(residue_mask, blk_place * block_rows, block_rows).astype(
        jnp.float32
    )
    weight = (rows_valid[:, None] * res_valid[None, :])[:, :, None]
    left_matrix = (
        jnp.einsum("sic,cd->sid", normed, lower_weights, preferred_element_type=jnp.float32)
        * weight
    ).astype(jnp.bfloat16)
    right = (
        jnp.einsum("sic,cd->sid", normed, upper_weights, preferred_element_type=jnp.float32)
        * weight
    ).astype(jnp.bfloat16)
    right_flat = right.reshape(local_rows, block_rows * proj_width)
    table = output_projector.reshape(proj_width, proj_width, pair_width)
    out_width = pair_width // core_count
    table_used = lax.dynamic_slice_in_dim(table, core_place * out_width, out_width, 2)
    used_channels = table_used.shape[2]
    piece = lax.all_gather(right_flat, "blk", axis=1, tiled=True)
    col_count = piece.shape[1] // proj_width
    block_cols = math.gcd(col_count, 128)
    block_count = col_count // block_cols
    stacked = piece.reshape(local_rows, block_count, block_cols, proj_width).transpose(1, 0, 2, 3)

    def one_block(right_part):
        outer = jnp.einsum(
            "sic,sjd->ijcd", left_matrix, right_part, preferred_element_type=jnp.float32
        ).astype(jnp.bfloat16)
        return jnp.einsum("ijcd,cde->eij", outer, table_used, preferred_element_type=jnp.float32)

    results = lax.map(one_block, stacked)
    partial_sum = results.transpose(1, 2, 0, 3).reshape(used_channels, block_rows, col_count)
    all_cols = partial_sum.shape[2]
    quarter_cols = all_cols // seq_count
    summed = lax.psum_scatter(
        partial_sum.astype(jnp.bfloat16), "seq", scatter_dimension=2, tiled=True
    ).astype(jnp.float32)
    count = jnp.sum(sequence_mask.astype(jnp.float32))
    col_valid = lax.dynamic_slice_in_dim(
        residue_mask, seq_place * quarter_cols, quarter_cols
    ).astype(jnp.float32)
    norm = res_valid[:, None] * col_valid[None, :] * count
    return (summed / jnp.maximum(norm, 1.0)[None]).astype(jnp.bfloat16)


def solution(mesh):
    in_specs = (P(("grp", "seq"), "blk", None), P("grp"), P("grp"), P(), P(), P())
    out_specs = P("ch", ("grp", "blk"), "seq")
    return jax.shard_map(shards, mesh=mesh, in_specs=in_specs, out_specs=out_specs, check_vma=False)
```

profile of v0, /device:TPU:0, one launch (start us, length us, event | category | flops | bytes accessed | tf_op | source)
XLA Modules:
  0.0 110.0 jit_solution(18392558506096459744)
XLA Ops:
  6.5 0.0 copy-start
  6.5 0.0 all-gather.2.cloned.1.call-start
  6.5 1.2 %convert_reduce_fusion = f32[256,16]{0,1:T(8,128)S(1)} fusion(bf16[256,16,64]{0,2,1:T(8,128)(2,1)} %param.6), kind=kLoop, calls=%fused_computation.4 | loop fusion | flops 520192 | bytes 540672 | tf_op jit(solution)/shard_map/reduce_sum | solution.py:20
  7.7 1.2 %fusion.23 = f32[256,16]{0,1:T(8,128)S(1)} fusion(bf16[256,16,64]{0,2,1:T(8,128)(2,1)} %param.6, f32[256,16]{0,1:T(8,128)S(1)} %broadcast_multiply_fusion.1), kind=kLoop, calls=%fused_computation.17 | loop fusion | flops 1044480 | bytes 557056 | tf_op jit(solution)/shard_map/reduce_sum | solution.py:21
  8.9 0.7 convert_element_type.40
  9.6 0.7 dynamic-slice_convert_fusion
  10.4 0.1 add_rsqrt_fusion
  10.4 2.0 %fusion.20 = bf16[256,16,32]{0,2,1:T(8,128)(2,1)} fusion(bf16[256,16,64]{0,2,1:T(8,128)(2,1)} %param.6, f32[256,16]{0,1:T(8,128)S(1)} %get-tuple-element.13, f32[256,16]{0,1:T(8,128)S(1)} %broadcast_multiply_fusion.1, f32[256,16]{0,1:T(8,128)S(1)} %get-tuple-element.14, bf16[64,32]{0,1:T(8,128)(2,1)} %param.10), kind=kOutput, calls=%fused_computation.14 | convolution fusion | flops 18087936 | bytes 839680 | tf_op jit(solution)/shard_map/sic,cd->sid/dot_general | solution.py:35
  12.5 0.0 all-gather.2.cloned.1.call-update
  12.5 0.7 convert_element_type.48
  13.1 1.4 %convert_reduce_fusion.1 = f32[]{:T(128)} fusion(s32[256]{0:T(256)} %param.7), kind=kLoop, calls=%fused_computation.31 | loop fusion | flops 511 | bytes 1028 | tf_op jit(solution)/shard_map/reduce_sum | solution.py:62
  14.5 0.8 multiply_maximum_fusion
  15.3 49.4 %all-gather.2.cloned.1.call-done = bf16[256,4096]{0,1:T(8,128)(2,1)} async-done(((bf16[256,512]{0,1:T(8,128)(2,1)}), bf16[256,4096]{0,1:T(8,128)(2,1)}) %all-gather.2.cloned.1.call-update) | async-done | bytes 2097168 | tf_op jit(solution)/shard_map/all_gather | solution.py:43
  64.6 9.9 %fusion.25 = bf16[128,32,16,32]{3,1,2,0:T(8,128)(2,1)} fusion(bf16[256,128,32,1]{0,2,3,1:T(8,128)(2,1)} %bitcast.47, bf16[256,16,64]{0,2,1:T(8,128)(2,1)} %param.6, f32[256,16]{0,1:T(8,128)S(1)} %get-tuple-element.13, f32[256,16]{0,1:T(8,128)S(1)} %broadcast_multiply_fusion.1, f32[256,16]{0,1:T(8,128)S(1)} %get-tuple-element.14, bf16[64,32]{0,1:T(8,128)(2,1)} %param.9), kind=kOutput, calls=%fused_computation.19 | convolution fusion | flops 1091829760 | bytes 6868992 | tf_op jit(solution)/shard_map/while/body/eval_jaxpr/sic,sjd->ijcd/dot_general | solution.py:50
  74.6 24.6 %copy.9 = bf16[128,32,16,32]{0,1,3,2:T(8,128)(2,1)} copy(bf16[128,32,16,32]{3,1,2,0:T(8,128)(2,1)} %fusion.25) | data formatting | bytes 8388608 | tf_op jit(solution)/shard_map/while/body/eval_jaxpr/sic,sjd->ijcd/dot_general | solution.py:50
  99.2 0.0 copy-done
  99.2 3.1 %fusion.17 = bf16[64,16,128]{2,0,1:T(8,128)(2,1)S(1)} fusion(bf16[128,32,16,32]{0,1,3,2:T(8,128)(2,1)} %copy.9, f32[16,128]{1,0:T(8,128)S(1)} %multiply_maximum_fusion, bf16[32,32,128]{2,1,0:T(8,128)(2,1)S(1)} %bitcast.46, s32[]{:T(128)S(6)} %select_n.8), kind=kOutput, calls=%fused_computation.13 | convolution fusion | flops 268959744 | bytes 4726788 | tf_op jit(solution)/shard_map/while/body/eval_jaxpr/ijcd,cde->eij/dot_general | solution.py:53
  102.3 0.9 copy.7
  (1 shorter events, 0.0 us)
Async XLA Ops:
  6.5 92.6 %copy-start = (bf16[1024,128]{1,0:T(8,128)(2,1)S(1)}, bf16[1024,128]{1,0:T(8,128)(2,1)}, u32[]{:S(2)}) copy-start(bf16[1024,128]{1,0:T(8,128)(2,1)} %param.11) | copy-start | bytes 786436
  6.5 58.1 %all-gather.2.cloned.1.call-start = ((), (), s32[]{:S(2)}) async-start(), calls=%async_computation | async-start | bytes 2359296 | tf_op jit(solution)/shard_map/all_gather | solution.py:43
Sparse Core Ops, SparseCore 0:
  12.6 51.9 all-gather.1
where the time goes:
time: 110 us
  waiting for transfers between devices  49.4 us (45%)
  local copies, waits for them, and re-layouts  25.5 us (23%)
  matrix products  15.1 us (14%)
  between operations  13.4 us (12%)
  other arithmetic  6.66 us (6%)
    all_gather x1, waiting for transfers between devices, shards(): piece = lax.all_gather(right_flat, 'blk', axis=1, tiled=True)  49.4 us
    dot_general x1, local copies, waits for them, and re-layouts, one_block(): jnp.einsum('sic,sjd->ijcd', left_matrix, right_part, preferred_element_ty...  24.6 us
    dot_general x1, matrix products, one_block(): jnp.einsum('sic,sjd->ijcd', left_matrix, right_part, preferred_element_ty...  9.94 us
    dot_general x1, matrix products, one_block(): jnp.einsum('ijcd,cde->eij', outer, table_used, preferred_element_type=jnp...  3.13 us
  transfers between devices with their start and end apart: 1, of which 1 were waited for; matrix products, arithmetic and copies ran while one was open for 3% of the time, Pallas kernels for 0%

commit v1 on v0

--- a/solution.py
+++ b/solution.py
@@ -1,8 +1,27 @@
+import functools
 import math
 import jax
 import jax.numpy as jnp
 from jax import lax
 from jax.sharding import PartitionSpec as P
+
+
+def link_the_rails(v0, net_axis):
+    slots = lax.axis_size(net_axis)
+    r1 = range(slots)
+    big = map(lambda tick: (tick, (tick + 1) % slots), r1)
+    frames = list(big)
+    next_value = [None] * slots
+    next_value[slots - 1] = v0
+    for nth in range(slots - 2, -1, -1):
+        next_value[nth] = lax.ppermute(next_value[nth + 1], net_axis, frames)
+    e_next = jnp.concatenate(next_value, 1)
+    vec_out = lax.axis_index(net_axis)
+    extra = (vec_out + 1) * v0.shape[1]
+    return jnp.roll(e_next, extra, 1)
+
+
+prepare_core = functools.partial(link_the_rails, net_axis="blk")
 
 
 def shards(
@@ -40,7 +59,7 @@
     out_width = pair_width // core_count
     table_used = lax.dynamic_slice_in_dim(table, core_place * out_width, out_width, 2)
     used_channels = table_used.shape[2]
-    piece = lax.all_gather(right_flat, "blk", axis=1, tiled=True)
+    piece = prepare_core(right_flat)
     col_count = piece.shape[1] // proj_width
     block_cols = math.gcd(col_count, 128)
     block_count = col_count // block_cols

time: 110 us -> 112 us (1.018)
  waiting for transfers between devices: 49.4 us -> 63.1 us
  between operations: 13.4 us -> 0.19 us
  starting transfers between devices: 0.01 us -> 3.01 us
  matrix products: 15.1 us -> 12.7 us
    ppermute x0 -> x7, waiting for transfers between devices: none -> 63.1 us  [link_the_rails(): next_value[nth] = lax.ppermute(next_value[nth + 1], net_axis, frames)]
    all_gather x1 -> x0, waiting for transfers between devices: 49.4 us -> none  [shards(): piece = lax.all_gather(right_flat, 'blk', axis=1, tiled=True)]
    ppermute x0 -> x7, starting transfers between devices: none -> 3.01 us  [link_the_rails(): next_value[nth] = lax.ppermute(next_value[nth + 1], net_axis, frames)]
    dot_general x1, matrix products: 9.94 us -> 8.23 us  [one_block(): jnp.einsum('sic,sjd->ijcd', left_matrix, right_part, preferred_element_ty...]
  transfers between devices with their start and end apart: 1 -> 7, of which waited for: 1 -> 7; matrix products, arithmetic and copies ran while one was open for 3% -> 2% of each run, Pallas kernels for 0% -> 0%
where the time goes in v1:
time: 112 us
  waiting for transfers between devices  63.1 us (56%)
  local copies, waits for them, and re-layouts  26.6 us (24%)
  matrix products  12.7 us (11%)
  other arithmetic  6.54 us (6%)
  starting transfers between devices  3.01 us (3%)
    ppermute x7, waiting for transfers between devices, link_the_rails(): next_value[nth] = lax.ppermute(next_value[nth + 1], net_axis, frames)  63.1 us
    dot_general x1, local copies, waits for them, and re-layouts, one_block(): jnp.einsum('sic,sjd->ijcd', left_matrix, right_part, preferred_element_ty...  24.6 us
    dot_general x1, matrix products, one_block(): jnp.einsum('sic,sjd->ijcd', left_matrix, right_part, preferred_element_ty...  8.23 us
    dot_general x1, matrix products, one_block(): jnp.einsum('ijcd,cde->eij', outer, table_used, preferred_element_type=jnp...  3.13 us
    ppermute x7, starting transfers between devices, link_the_rails(): next_value[nth] = lax.ppermute(next_value[nth + 1], net_axis, frames)  3.01 us
  transfers between devices with their start and end apart: 7, of which 7 were waited for; matrix products, arithmetic and copies ran while one was open for 2% of the time, Pallas kernels for 0%

profile of v1, /device:TPU:0, one launch (start us, length us, event | category | flops | bytes accessed | tf_op | source)
XLA Modules:
  0.0 112.0 jit_solution(7083999207629955469)
XLA Ops:
  0.0 0.0 copy-start
  0.0 1.2 %convert_reduce_fusion = f32[256,16]{0,1:T(8,128)S(1)} fusion(bf16[256,16,64]{0,2,1:T(8,128)(2,1)} %param.6), kind=kLoop, calls=%fused_computation.4 | loop fusion | flops 520192 | bytes 540672 | tf_op jit(solution)/shard_map/reduce_sum | solution.py:39
  1.2 1.2 %fusion.23 = f32[256,16]{0,1:T(8,128)S(1)} fusion(bf16[256,16,64]{0,2,1:T(8,128)(2,1)} %param.6, f32[256,16]{0,1:T(8,128)S(1)} %broadcast_multiply_fusion.1), kind=kLoop, calls=%fused_computation.17 | loop fusion | flops 1044480 | bytes 557056 | tf_op jit(solution)/shard_map/reduce_sum | solution.py:40
  2.4 0.7 convert_element_type.40
  3.1 0.7 dynamic-slice_convert_fusion
  3.8 0.1 add_rsqrt_fusion
  3.9 1.3 %fusion.20 = bf16[256,16,32]{0,2,1:T(8,128)(2,1)S(1)} fusion(bf16[256,16,64]{0,2,1:T(8,128)(2,1)} %param.6, f32[256,16]{0,1:T(8,128)S(1)} %get-tuple-element.13, f32[256,16]{0,1:T(8,128)S(1)} %broadcast_multiply_fusion.1, f32[256,16]{0,1:T(8,128)S(1)} %get-tuple-element.14, bf16[64,32]{0,1:T(8,128)(2,1)} %param.10), kind=kOutput, calls=%fused_computation.14 | convolution fusion | flops 18087936 | bytes 839680 | tf_op jit(solution)/shard_map/sic,cd->sid/dot_general | solution.py:54
  5.2 3.0 %collective-permute-start = (bf16[256,512]{0,1:T(8,128)(2,1)S(1)}, bf16[256,512]{0,1:T(8,128)(2,1)S(1)}, u32[]{:S(2)}, u32[]{:S(2)}) collective-permute-start(bf16[256,512]{0,1:T(8,128)(2,1)S(1)} %bitcast.48), channel_id=1, source_target_pairs={{0,2},{2,4},{4,6},{6,8},{8,10},{10,12},{12,14},{14,0},{1,3},{3,5},... | collective-permute-start | bytes 786440 | tf_op jit(solution)/shard_map/ppermute | solution.py:17
  8.2 9.3 %collective-permute-done = bf16[256,512]{0,1:T(8,128)(2,1)S(1)} collective-permute-done((bf16[256,512]{0,1:T(8,128)(2,1)S(1)}, bf16[256,512]{0,1:T(8,128)(2,1)S(1)}, u32[]{:S(2)}, u32[]{:S(2)}) %collective-permute-start) | collective-permute-done | bytes 262176 | tf_op jit(solution)/shard_map/ppermute | solution.py:17
  17.6 0.0 collective-permute-start.1
  17.6 10.2 %collective-permute-done.1 = bf16[256,512]{0,1:T(8,128)(2,1)S(1)} collective-permute-done((bf16[256,512]{0,1:T(8,128)(2,1)S(1)}, bf16[256,512]{0,1:T(8,128)(2,1)S(1)}, u32[]{:S(2)}, u32[]{:S(2)}) %collective-permute-start.1) | collective-permute-done | bytes 262176 | tf_op jit(solution)/shard_map/ppermute | solution.py:17
  27.8 0.0 collective-permute-start.2
  27.8 9.3 %collective-permute-done.2 = bf16[256,512]{0,1:T(8,128)(2,1)S(1)} collective-permute-done((bf16[256,512]{0,1:T(8,128)(2,1)S(1)}, bf16[256,512]{0,1:T(8,128)(2,1)S(1)}, u32[]{:S(2)}, u32[]{:S(2)}) %collective-permute-start.2) | collective-permute-done | bytes 262176 | tf_op jit(solution)/shard_map/ppermute | solution.py:17
  37.0 0.0 collective-permute-start.3
  37.0 9.1 %collective-permute-done.3 = bf16[256,512]{0,1:T(8,128)(2,1)S(1)} collective-permute-done((bf16[256,512]{0,1:T(8,128)(2,1)S(1)}, bf16[256,512]{0,1:T(8,128)(2,1)S(1)}, u32[]{:S(2)}, u32[]{:S(2)}) %collective-permute-start.3) | collective-permute-done | bytes 262176 | tf_op jit(solution)/shard_map/ppermute | solution.py:17
  46.1 0.0 collective-permute-start.4
  46.1 9.1 %collective-permute-done.4 = bf16[256,512]{0,1:T(8,128)(2,1)S(1)} collective-permute-done((bf16[256,512]{0,1:T(8,128)(2,1)S(1)}, bf16[256,512]{0,1:T(8,128)(2,1)S(1)}, u32[]{:S(2)}, u32[]{:S(2)}) %collective-permute-start.4) | collective-permute-done | bytes 262176 | tf_op jit(solution)/shard_map/ppermute | solution.py:17
  55.2 0.0 collective-permute-start.5
  55.2 9.7 %collective-permute-done.5 = bf16[256,512]{0,1:T(8,128)(2,1)S(1)} collective-permute-done((bf16[256,512]{0,1:T(8,128)(2,1)S(1)}, bf16[256,512]{0,1:T(8,128)(2,1)S(1)}, u32[]{:S(2)}, u32[]{:S(2)}) %collective-permute-start.5) | collective-permute-done | bytes 262176 | tf_op jit(solution)/shard_map/ppermute | solution.py:17
  64.9 0.0 collective-permute-start.6
  64.9 1.3 %convert_reduce_fusion.1 = f32[]{:T(128)} fusion(s32[256]{0:T(256)} %param.7), kind=kLoop, calls=%fused_computation.48 | loop fusion | flops 511 | bytes 1028 | tf_op jit(solution)/shard_map/reduce_sum | solution.py:81
  66.2 0.7 convert_element_type.48
  66.8 0.7 multiply_maximum_fusion
  67.5 6.4 %collective-permute-done.6 = bf16[256,512]{0,1:T(8,128)(2,1)S(1)} collective-permute-done((bf16[256,512]{0,1:T(8,128)(2,1)S(1)}, bf16[256,512]{0,1:T(8,128)(2,1)S(1)}, u32[]{:S(2)}, u32[]{:S(2)}) %collective-permute-start.6) | collective-permute-done | bytes 262176 | tf_op jit(solution)/shard_map/ppermute | solution.py:17
  74.2 0.0 copy-start.1
  74.2 0.0 copy-start.2
  74.4 0.1 constant_dynamic-slice_fusion
  74.6 0.6 copy-done.1
  75.2 0.0 copy-done.2
  75.2 8.2 %fusion.25 = bf16[128,32,16,32]{3,1,2,0:T(8,128)(2,1)} fusion(bf16[256,128,32,1]{0,2,3,1:T(8,128)(2,1)S(1)} %bitcast.47, bf16[256,16,64]{0,2,1:T(8,128)(2,1)S(1)} %copy-done.1, f32[256,16]{0,1:T(8,128)S(1)} %get-tuple-element.13, f32[256,16]{0,1:T(8,128)S(1)} %broadcast_multiply_fusion.1, f32[256,16]{0,1:T(8,128)S(1)} %get-tuple-element.14, ...), kind=kOutput, calls=%fused_computation.19 | convolution fusion | flops 1091829760 | bytes 6868992 | tf_op jit(solution)/shard_map/while/body/eval_jaxpr/sic,sjd->ijcd/dot_general | solution.py:69
  83.4 24.6 %copy.9 = bf16[128,32,16,32]{0,1,3,2:T(8,128)(2,1)} copy(bf16[128,32,16,32]{3,1,2,0:T(8,128)(2,1)} %fusion.25) | data formatting | bytes 8388608 | tf_op jit(solution)/shard_map/while/body/eval_jaxpr/sic,sjd->ijcd/dot_general | solution.py:69
  108.0 0.0 copy-done
  108.0 3.1 %fusion.17 = bf16[64,16,128]{2,0,1:T(8,128)(2,1)S(1)} fusion(bf16[128,32,16,32]{0,1,3,2:T(8,128)(2,1)} %copy.9, f32[16,128]{1,0:T(8,128)S(1)} %multiply_maximum_fusion, bf16[32,32,128]{2,1,0:T(8,128)(2,1)S(1)} %bitcast.46, s32[]{:T(128)S(6)} %select_n.21), kind=kOutput, calls=%fused_computation.13 | convolution fusion | flops 268959744 | bytes 4726788 | tf_op jit(solution)/shard_map/while/body/eval_jaxpr/ijcd,cde->eij/dot_general | solution.py:72
  111.1 0.9 copy.7
  (17 shorter events, 0.3 us)
Async XLA Ops:
  0.0 108.0 %copy-start = (bf16[1024,128]{1,0:T(8,128)(2,1)S(1)}, bf16[1024,128]{1,0:T(8,128)(2,1)}, u32[]{:S(2)}) copy-start(bf16[1024,128]{1,0:T(8,128)(2,1)} %param.11) | copy-start | bytes 786436
  5.2 12.3 %collective-permute-start = (bf16[256,512]{0,1:T(8,128)(2,1)S(1)}, bf16[256,512]{0,1:T(8,128)(2,1)S(1)}, u32[]{:S(2)}, u32[]{:S(2)}) collective-permute-start(bf16[256,512]{0,1:T(8,128)(2,1)S(1)} %bitcast.48), channel_id=1, source_target_pairs={{0,2},{2,4},{4,6},{6,8},{8,10},{10,12},{12,14},{14,0},{1,3},{3,5},... | collective-permute-start | bytes 786440 | tf_op jit(solution)/shard_map/ppermute | solution.py:17
  17.6 10.2 %collective-permute-start.1 = (bf16[256,512]{0,1:T(8,128)(2,1)S(1)}, bf16[256,512]{0,1:T(8,128)(2,1)S(1)}, u32[]{:S(2)}, u32[]{:S(2)}) collective-permute-start(bf16[256,512]{0,1:T(8,128)(2,1)S(1)} %collective-permute-done), channel_id=1, source_target_pairs={{0,2},{2,4},{4,6},{6,8},{8,10},{10,12},{12,14},{14,0},{1,3},{3,5},... | collective-permute-start | bytes 786440 | tf_op jit(solution)/shard_map/ppermute | solution.py:17
  27.8 9.3 %collective-permute-start.2 = (bf16[256,512]{0,1:T(8,128)(2,1)S(1)}, bf16[256,512]{0,1:T(8,128)(2,1)S(1)}, u32[]{:S(2)}, u32[]{:S(2)}) collective-permute-start(bf16[256,512]{0,1:T(8,128)(2,1)S(1)} %collective-permute-done.1), channel_id=1, source_target_pairs={{0,2},{2,4},{4,6},{6,8},{8,10},{10,12},{12,14},{14,0},{1,3},{3,5},... | collective-permute-start | bytes 786440 | tf_op jit(solution)/shard_map/ppermute | solution.py:17
  37.0 9.1 %collective-permute-start.3 = (bf16[256,512]{0,1:T(8,128)(2,1)S(1)}, bf16[256,512]{0,1:T(8,128)(2,1)S(1)}, u32[]{:S(2)}, u32[]{:S(2)}) collective-permute-start(bf16[256,512]{0,1:T(8,128)(2,1)S(1)} %collective-permute-done.2), channel_id=1, source_target_pairs={{0,2},{2,4},{4,6},{6,8},{8,10},{10,12},{12,14},{14,0},{1,3},{3,5},... | collective-permute-start | bytes 786440 | tf_op jit(solution)/shard_map/ppermute | solution.py:17
  46.1 9.1 %collective-permute-start.4 = (bf16[256,512]{0,1:T(8,128)(2,1)S(1)}, bf16[256,512]{0,1:T(8,128)(2,1)S(1)}, u32[]{:S(2)}, u32[]{:S(2)}) collective-permute-start(bf16[256,512]{0,1:T(8,128)(2,1)S(1)} %collective-permute-done.3), channel_id=1, source_target_pairs={{0,2},{2,4},{4,6},{6,8},{8,10},{10,12},{12,14},{14,0},{1,3},{3,5},... | collective-permute-start | bytes 786440 | tf_op jit(solution)/shard_map/ppermute | solution.py:17
  55.2 9.7 %collective-permute-start.5 = (bf16[256,512]{0,1:T(8,128)(2,1)S(1)}, bf16[256,512]{0,1:T(8,128)(2,1)S(1)}, u32[]{:S(2)}, u32[]{:S(2)}) collective-permute-start(bf16[256,512]{0,1:T(8,128)(2,1)S(1)} %collective-permute-done.4), channel_id=1, source_target_pairs={{0,2},{2,4},{4,6},{6,8},{8,10},{10,12},{12,14},{14,0},{1,3},{3,5},... | collective-permute-start | bytes 786440 | tf_op jit(solution)/shard_map/ppermute | solution.py:17
  64.9 9.1 %collective-permute-start.6 = (bf16[256,512]{0,1:T(8,128)(2,1)S(1)}, bf16[256,512]{0,1:T(8,128)(2,1)S(1)}, u32[]{:S(2)}, u32[]{:S(2)}) collective-permute-start(bf16[256,512]{0,1:T(8,128)(2,1)S(1)} %collective-permute-done.5), channel_id=1, source_target_pairs={{0,2},{2,4},{4,6},{6,8},{8,10},{10,12},{12,14},{14,0},{1,3},{3,5},... | collective-permute-start | bytes 786440 | tf_op jit(solution)/shard_map/ppermute | solution.py:17
  74.2 1.0 copy-start.1
  74.2 1.0 copy-start.2
